TPU v7x, 32 devices: a whole 2x2x4 slice. The times are simulated.
32 devices in a mesh: seq: 8 (over z, y), feat: 4 (over x, core).
Axes of the slice: x: 2, y: 2, z: 4, core: 2. Of those that a mesh axis runs over, the one named last changes fastest.
Arguments:
- activations_in: bfloat16 [6144, 512], P('seq', 'feat'), may hold values from -6 to 6
- cotangent: bfloat16 [6144, 512], P('seq', 'feat'), may hold values from -6 to 6
- seq_start: int32 [16], P('seq'), may hold values from 0 to 768, as said below
- seq_length: int32 [16], P('seq'), may hold values from 0 to 768, as said below
- input_matrix: float32 [2, 512, 768], P(None, 'feat'), may hold values from -0.25 to 0.25
- output_matrix: float32 [2, 1536, 512], P(None, None, 'feat'), may hold values from -1.25 to 1.25
- gate_matrix: float32 [2, 512, 512], P(None, None, 'feat'), may hold values from -0.25 to 0.25
- feature_vectors: float32 [2, 4, 512], P(None, None, 'feat'), may hold values from 0.1 to 1.9
- state_vectors: float32 [2, 3, 384], replicated, may hold values from -20 to 20, as said below
- velocity_input: float32 [2, 512, 768], P(None, 'feat'), may hold values from -6 to 6
- velocity_output: float32 [2, 1536, 512], P(None, None, 'feat'), may hold values from -6 to 6
- velocity_gate: float32 [2, 512, 512], P(None, None, 'feat'), may hold values from -6 to 6
- velocity_feature: float32 [2, 4, 512], P(None, None, 'feat'), may hold values from -6 to 6
- velocity_state: float32 [2, 3, 384], replicated, may hold values from -6 to 6
- average_input: float32 [2, 512, 768], P(None, 'feat'), may hold values from -0.25 to 0.25
- average_output: float32 [2, 1536, 512], P(None, None, 'feat'), may hold values from -1.25 to 1.25
- average_gate: float32 [2, 512, 512], P(None, None, 'feat'), may hold values from -0.25 to 0.25
- average_feature: float32 [2, 4, 512], P(None, None, 'feat'), may hold values from 0.1 to 1.9
- average_state: float32 [2, 3, 384], replicated, may hold values from -3 to 1
Outputs:
- activations_out: float32 [6144, 512], P('seq', 'feat')
- input_gradient: float32 [6144, 512], P('seq', 'feat')
- gradient_input: float32 [2, 512, 768], P(None, 'feat')
- gradient_output: float32 [2, 1536, 512], P(None, None, 'feat')
- gradient_gate: float32 [2, 512, 512], P(None, None, 'feat')
- gradient_feature: float32 [2, 4, 512], P(None, None, 'feat')
- gradient_state: float32 [2, 3, 384], replicated
- updated_input: float32 [2, 512, 768], P(None, 'feat')
- updated_output: float32 [2, 1536, 512], P(None, None, 'feat')
- updated_gate: float32 [2, 512, 512], P(None, None, 'feat')
- updated_feature: float32 [2, 4, 512], P(None, None, 'feat')
- state_change: float32 [2, 3, 384], replicated
- momentum_input: float32 [2, 512, 768], P(None, 'feat')
- momentum_output: float32 [2, 1536, 512], P(None, None, 'feat')
- momentum_gate: float32 [2, 512, 512], P(None, None, 'feat')
- momentum_feature: float32 [2, 4, 512], P(None, None, 'feat')
- momentum_state: float32 [2, 3, 384], replicated
- smoothed_input: float32 [2, 512, 768], P(None, 'feat')
- smoothed_output: float32 [2, 1536, 512], P(None, None, 'feat')
- smoothed_gate: float32 [2, 512, 512], P(None, None, 'feat')
- smoothed_feature: float32 [2, 4, 512], P(None, None, 'feat')
- smoothed_state: float32 [2, 3, 384], replicated
Inputs may be any that keep to these rules, and one draw needn't show every extreme that they name: `seq_length`: sequences of a device lie in its own buffer, ordered and without intersection; one device holds a single sequence of 768 tokens and an empty slot, every other device two sequences of 192 to 384 tokens. `seq_start`: positions within a device's buffer; a slot of length zero starts at 768. `state_vectors`: rows hold log(-Re Lambda), Im Lambda and the log timestep.
All inputs are finite; a program needn't handle non-finite values.
Results may differ from a plain program's by a relative error of at most 0.012.
The roundings to bfloat16 on the way count: a program that leaves them out, or rounds other values in their place, can miss the bound.
Values may be sent and summed in bfloat16 or wider, within the bound.
A program may use at most 448 MiB of HBM per device.

v0:
```python
import math
import jax
import jax.numpy as jnp
from jax import lax
from jax.sharding import PartitionSpec as P

epsilon = 1e-05
momentum = 0.9
smoothing = 0.5
slow_rate = 0.02
main_rate = 0.05
weight_decay = 0.1


def smooth(value):
    return jax.nn.gelu(value, approximate=False)


def combine(earlier, later):
    mult_real = later[0] * earlier[0] - later[1] * earlier[1]
    mult_imag = later[0] * earlier[1] + later[1] * earlier[0]
    add_real = later[0] * earlier[2] - later[1] * earlier[3] + later[2]
    add_imag = later[0] * earlier[3] + later[1] * earlier[2] + later[3]
    return (mult_real, mult_imag, add_real, add_imag)


def masks_of(starts, lengths, count):
    position = jnp.arange(count, dtype=jnp.int32)[:, None]
    begin = starts[None, :]
    finish = begin + lengths[None, :]
    inside = (position >= begin) & (position < finish)
    alive = jnp.any(inside, 1)
    opening = jnp.any(inside & (position == begin), 1)
    closing = jnp.any(inside & (position == finish - 1), 1)
    return (
        alive.astype(jnp.float32),
        (alive & ~opening).astype(jnp.float32),
        (alive & ~closing).astype(jnp.float32),
    )


def prefix(current, backward):
    length = current[2].shape[0]
    offset = 1
    while offset < length:

        def shifted(value):
            filler = jnp.zeros((offset,) + value.shape[1:], value.dtype)
            if backward:
                return jnp.concatenate([value[offset:], filler], 0)
            return jnp.concatenate([filler, value[: length - offset]], 0)

        earlier = tuple((shifted(value) for value in current))
        current = combine(earlier, current)
        offset = offset * 2
    return current


def scan_states(drive, state_row, alive, carry_prev, carry_next):
    width = state_row.shape[1]
    rate = -jnp.exp(state_row[0])
    frequency = state_row[1]
    timestep = jnp.exp(state_row[2])
    decay = jnp.exp(rate * timestep)
    angle = frequency * timestep
    pole_real = decay * jnp.cos(angle)
    pole_imag = decay * jnp.sin(angle)
    denom = rate * rate + frequency * frequency
    factor_real = ((pole_real - 1.0) * rate + pole_imag * frequency) / denom
    factor_imag = (pole_imag * rate - (pole_real - 1.0) * frequency) / denom
    drive_real = drive[:, :width]
    drive_imag = drive[:, width:]
    input_real = (drive_real * factor_real - drive_imag * factor_imag) * alive[:, None]
    input_imag = (drive_real * factor_imag + drive_imag * factor_real) * alive[:, None]
    ahead = prefix(
        (carry_prev[:, None] * pole_real, carry_prev[:, None] * pole_imag, input_real, input_imag),
        False,
    )
    behind = prefix(
        (carry_next[:, None] * pole_real, carry_next[:, None] * pole_imag, input_real, input_imag),
        True,
    )
    return jnp.concatenate([ahead[2], ahead[3], behind[2], behind[3]], 1)


def update(weight, gradient, velocity, average, rate, decay):
    adjusted = gradient + decay * weight
    velocity_new = momentum * velocity + adjusted
    change = -rate * (adjusted + momentum * velocity_new)
    weight_new = weight + change
    average_new = smoothing * average + (1.0 - smoothing) * weight_new
    return (weight_new, velocity_new, average_new, change)


def contract_rows(left, right):
    return lax.dot_general(
        left, right, (((0,), (0,)), ((), ())), preferred_element_type=jnp.float32
    )


def contract_cols(left, right):
    return lax.dot_general(
        left, right, (((1,), (1,)), ((), ())), preferred_element_type=jnp.float32
    )


def moments(stream):
    whole = lax.all_gather(stream, "feat", axis=1, tiled=True)
    center = jnp.mean(whole, 1, keepdims=True)
    spread = whole - center
    variance = jnp.mean(spread * spread, 1, keepdims=True)
    return (center, lax.rsqrt(variance + epsilon))


def back_moments(unit_grad, unit):
    spread_grad, crossed = (
        lax.all_gather(unit_grad, "feat", axis=1, tiled=True),
        lax.all_gather(unit_grad * unit, "feat", axis=1, tiled=True),
    )
    return (jnp.mean(spread_grad, 1, keepdims=True), jnp.mean(crossed, 1, keepdims=True))


def state_forward(normed_low, in_low, state_row, masks):
    partial_drive = jnp.dot(normed_low, in_low, preferred_element_type=jnp.float32)
    drive = lax.psum(partial_drive, "feat")
    states = scan_states(drive, state_row, masks[0], masks[1], masks[2])
    return (drive, states.astype(jnp.bfloat16))


def state_backward(drive, state_row, masks, mixed_low, out_low):

    def scanned(drive_in, rows_in):
        return scan_states(drive_in, rows_in, masks[0], masks[1], masks[2])

    partial_states = contract_cols(mixed_low, out_low)
    states_grad = lax.psum(partial_states, "feat")
    unused, pull = jax.vjp(scanned, drive, state_row)
    drive_grad, row_grad = pull(states_grad)
    return (drive_grad.astype(jnp.bfloat16), row_grad)


def body(
    activations_in,
    cotangent,
    seq_start,
    seq_length,
    input_matrix,
    output_matrix,
    gate_matrix,
    feature_vectors,
    state_vectors,
    velocity_input,
    velocity_output,
    velocity_gate,
    velocity_feature,
    velocity_state,
    average_input,
    average_output,
    average_gate,
    average_feature,
    average_state,
):
    count = activations_in.shape[0]
    layers = input_matrix.shape[0]
    masks = masks_of(seq_start, seq_length, count)
    stream = activations_in.astype(jnp.float32)
    saved = []
    for layer in range(layers):
        in_low = input_matrix[layer].astype(jnp.bfloat16)
        out_low = output_matrix[layer].astype(jnp.bfloat16)
        gate_low = gate_matrix[layer].astype(jnp.bfloat16)
        feature_row = feature_vectors[layer]
        center, scale = moments(stream)
        unit = (stream - center) * scale
        normed = unit * feature_row[0] + feature_row[1]
        normed_low = normed.astype(jnp.bfloat16)
        drive, states_low = state_forward(normed_low, in_low, state_vectors[layer], masks)
        mixed = (
            jnp.dot(states_low, out_low, preferred_element_type=jnp.float32)
            + feature_row[2] * normed
        )
        act = smooth(mixed)
        act_all = lax.all_gather(act.astype(jnp.bfloat16), "feat", axis=1, tiled=True)
        pre = jnp.dot(act_all, gate_low, preferred_element_type=jnp.float32) + feature_row[3]
        saved.append((scale, unit, normed, normed_low, drive, states_low, mixed, act, act_all, pre))
        stream = stream + act * jax.nn.sigmoid(pre)
    grad = cotangent.astype(jnp.float32) * masks[0][:, None]
    layer_grads = [None] * layers
    for layer in reversed(range(layers)):
        scale, unit, normed, normed_low, drive, states_low, mixed, act, act_all, pre = saved[layer]
        in_low = input_matrix[layer].astype(jnp.bfloat16)
        out_low = output_matrix[layer].astype(jnp.bfloat16)
        gate_low = gate_matrix[layer].astype(jnp.bfloat16)
        feature_row = feature_vectors[layer]
        gate = jax.nn.sigmoid(pre)
        pre_grad = (grad * act * gate * (1.0 - gate)).astype(jnp.bfloat16)
        gate_grad = contract_rows(act_all, pre_grad)
        gate_bias_grad = jnp.sum(pre_grad.astype(jnp.float32), 0)
        act_grad = grad * gate + lax.psum_scatter(
            contract_cols(pre_grad, gate_low), "feat", scatter_dimension=1, tiled=True
        )
        mixed_grad = jax.vjp(smooth, mixed)[1](act_grad)[0]
        skip_grad = jnp.sum(mixed_grad * normed, 0)
        mixed_low = mixed_grad.astype(jnp.bfloat16)
        out_grad = contract_rows(states_low, mixed_low)
        drive_low, row_grad = state_backward(drive, state_vectors[layer], masks, mixed_low, out_low)
        in_grad = contract_rows(normed_low, drive_low)
        normed_grad = mixed_grad * feature_row[2] + contract_cols(drive_low, in_low)
        gain_grad = jnp.sum(normed_grad * unit, 0)
        bias_grad = jnp.sum(normed_grad, 0)
        unit_grad = normed_grad * feature_row[0]
        first_mean, second_mean = back_moments(unit_grad, unit)
        grad = grad + scale * (unit_grad - first_mean - unit * second_mean)
        feature_grad = jnp.stack([gain_grad, bias_grad, skip_grad, gate_bias_grad])
        layer_grads[layer] = (in_grad, out_grad, gate_grad, feature_grad, row_grad)
    stacked_in = jnp.stack([entry[0] for entry in layer_grads])
    stacked_out = jnp.stack([entry[1] for entry in layer_grads])
    stacked_gate = jnp.stack([entry[2] for entry in layer_grads])
    stacked_feature = jnp.stack([entry[3] for entry in layer_grads])
    stacked_state = jnp.stack([entry[4] for entry in layer_grads])
    summed = lax.psum(
        (stacked_in, stacked_out, stacked_gate, stacked_feature, stacked_state), "seq"
    )
    factor = 1.0 / math.sqrt(count * lax.axis_size("seq"))
    grad_in = summed[0] * factor
    grad_out = summed[1] * factor
    grad_gate = summed[2] * factor
    grad_feature = summed[3] * factor
    grad_state = summed[4] * factor
    new_in = update(input_matrix, grad_in, velocity_input, average_input, slow_rate, 0.0)
    new_out = update(output_matrix, grad_out, velocity_output, average_output, slow_rate, 0.0)
    new_gate = update(gate_matrix, grad_gate, velocity_gate, average_gate, main_rate, weight_decay)
    new_feature = update(
        feature_vectors, grad_feature, velocity_feature, average_feature, main_rate, weight_decay
    )
    new_state = update(state_vectors, grad_state, velocity_state, average_state, slow_rate, 0.0)
    return (
        stream,
        grad,
        grad_in,
        grad_out,
        grad_gate,
        grad_feature,
        grad_state,
        new_in[0],
        new_out[0],
        new_gate[0],
        new_feature[0],
        new_state[3],
        new_in[1],
        new_out[1],
        new_gate[1],
        new_feature[1],
        new_state[1],
        new_in[2],
        new_out[2],
        new_gate[2],
        new_feature[2],
        new_state[2],
    )


def solution(mesh):
    return jax.shard_map(
        body,
        mesh=mesh,
        in_specs=(
            P("seq", "feat"),
            P("seq", "feat"),
            P("seq"),
            P("seq"),
            P(None, "feat", None),
            P(None, None, "feat"),
            P(None, None, "feat"),
            P(None, None, "feat"),
            P(),
            P(None, "feat", None),
            P(None, None, "feat"),
            P(None, None, "feat"),
            P(None, None, "feat"),
            P(),
            P(None, "feat", None),
            P(None, None, "feat"),
            P(None, None, "feat"),
            P(None, None, "feat"),
            P(),
        ),
        out_specs=(
            P("seq", "feat"),
            P("seq", "feat"),
            P(None, "feat", None),
            P(None, None, "feat"),
            P(None, None, "feat"),
            P(None, None, "feat"),
            P(),
            P(None, "feat", None),
            P(None, None, "feat"),
            P(None, None, "feat"),
            P(None, None, "feat"),
            P(),
            P(None, "feat", None),
            P(None, None, "feat"),
            P(None, None, "feat"),
            P(None, None, "feat"),
            P(),
            P(None, "feat", None),
            P(None, None, "feat"),
            P(None, None, "feat"),
            P(None, None, "feat"),
            P(),
        ),
        check_vma=False,
    )
```

profile of v0, /device:TPU:0, one launch (start us, length us, event | category | flops | bytes accessed | tf_op | source)
XLA Modules:
  0.0 1222.3 jit_solution(16966885579422786372)
XLA Ops:
  10.5 22.2 %all-gather.7.cloned.1.call-done = f32[768,512]{1,0:T(8,128)} async-done(((f32[768,128]{1,0:T(8,128)}), f32[768,512]{1,0:T(8,128)}) %all-gather.7.cloned.1.call-update) | async-done | bytes 1572880 | tf_op jit(solution)/shard_map/all_gather | solution.py:108
  36.7 3.1 fusion.344
  43.4 52.2 %all-reduce.322.cloned.1.call-done = f32[768,768]{1,0:T(8,128)} async-done(((f32[768,768]{1,0:T(8,128)}), f32[768,768]{1,0:T(8,128)}) %all-reduce.322.cloned.1.call-update) | async-done | bytes 2359312 | tf_op jit(solution)/shard_map/psum | solution.py:125
  103.3 2.9 subtract_add_fusion.23
  154.0 8.2 all_gather.25
  164.5 20.4 %all-gather.9.cloned.1.call-done = f32[768,512]{1,0:T(8,128)} async-done(((f32[768,128]{1,0:T(8,128)}), f32[768,512]{1,0:T(8,128)}) %all-gather.9.cloned.1.call-update) | async-done | bytes 1572880 | tf_op jit(solution)/shard_map/all_gather | solution.py:108
  188.8 3.1 fusion.345
  192.1 55.7 %all-reduce.324.cloned.1.call-done = f32[768,768]{1,0:T(8,128)} async-done(((f32[768,768]{1,0:T(8,128)}), f32[768,768]{1,0:T(8,128)}) %all-reduce.324.cloned.1.call-update) | async-done | bytes 2359312 | tf_op jit(solution)/shard_map/psum | solution.py:125
  256.6 3.1 subtract_add_fusion.11
  306.8 8.2 all_gather.27
  314.9 2.7 convert_reduce_fusion
  320.8 28.8 %reduce-scatter.3.cloned.1.call-done = f32[768,128]{1,0:T(8,128)} async-done(((f32[768,512]{1,0:T(8,128)}), f32[768,128]{1,0:T(8,128)}) %reduce-scatter.3.cloned.1.call-update) | async-done | bytes 393232 | tf_op jit(solution)/shard_map/reduce_scatter | solution.py:199
  352.9 3.9 fusion.341
  357.1 93.9 %all-reduce.326.cloned.1.call-done = f32[768,1536]{1,0:T(8,128)} async-done(((f32[768,1536]{1,0:T(8,128)}), f32[768,1536]{1,0:T(8,128)}) %all-reduce.326.cloned.1.call-update) | async-done | bytes 4718608 | tf_op jit(solution)/shard_map/psum | solution.py:136
  451.0 5.1 fusion.478
  456.1 2.9 fusion.328
  461.9 5.8 fusion.447
  467.7 3.6 fusion.502
  484.1 3.0 fusion.433
  494.6 4.0 fusion.445
  506.1 3.8 fusion.444
  517.8 4.0 fusion.432
  528.8 4.2 fusion.431
  541.2 3.4 fusion.443
  550.6 3.4 fusion.442
  562.2 3.8 fusion.430
  574.6 3.8 fusion.429
  586.3 4.0 fusion.441
  590.3 2.9 fusion.497
  599.9 4.0 fusion.440
  611.9 3.9 fusion.439
  622.0 3.7 multiply_reduce_fusion.3
  629.3 3.4 fusion.428
  645.8 3.5 multiply_reduce_fusion.2
  655.9 2.9 multiply_reduce_fusion.19
  659.7 19.4 %all-gather.13.cloned.1.call-done = f32[768,512]{1,0:T(8,128)} async-done(((f32[768,128]{1,0:T(8,128)}), f32[768,512]{1,0:T(8,128)}) %all-gather.13.cloned.1.call-update) | async-done | bytes 1572880 | tf_op jit(solution)/shard_map/all_gather | solution.py:118
  680.7 20.4 %all-gather.11.cloned.1.call-done = f32[768,512]{1,0:T(8,128)} async-done(((f32[768,128]{1,0:T(8,128)}), f32[768,512]{1,0:T(8,128)}) %all-gather.11.cloned.1.call-update) | async-done | bytes 1572880 | tf_op jit(solution)/shard_map/all_gather | solution.py:117
  707.7 28.3 %reduce-scatter.5.cloned.1.call-done = f32[768,128]{1,0:T(8,128)} async-done(((f32[768,512]{1,0:T(8,128)}), f32[768,128]{1,0:T(8,128)}) %reduce-scatter.5.cloned.1.call-update) | async-done | bytes 393232 | tf_op jit(solution)/shard_map/reduce_scatter | solution.py:199
  737.9 3.9 fusion.340
  742.3 93.7 %all-reduce.328.cloned.1.call-done = f32[768,1536]{1,0:T(8,128)} async-done(((f32[768,1536]{1,0:T(8,128)}), f32[768,1536]{1,0:T(8,128)}) %all-reduce.328.cloned.1.call-update) | async-done | bytes 4718608 | tf_op jit(solution)/shard_map/psum | solution.py:136
  836.0 4.8 fusion.477
  840.8 2.9 fusion.324
  846.5 5.0 fusion.423
  851.6 3.6 fusion.486
  867.6 3.4 fusion.409
  876.8 3.2 fusion.421
  885.6 3.4 fusion.420
  894.9 3.6 fusion.408
  904.8 3.9 fusion.407
  916.5 3.8 fusion.419
  928.0 3.8 fusion.418
  940.1 3.8 fusion.406
  952.5 3.9 fusion.405
  964.5 4.0 fusion.417
  968.5 2.9 fusion.481
  978.2 4.0 fusion.416
  990.1 3.9 fusion.415
  1000.2 3.0 multiply_reduce_fusion.11
  1006.9 3.4 fusion.404
  1023.3 2.9 multiply_reduce_fusion.10
  1032.8 2.9 multiply_reduce_fusion.21
  1049.8 37.1 %all-reduce.314 = (f32[2,4,128]{2,1,0:T(4,128)S(1)}, f32[2,3,384]{2,1,0:T(4,128)S(1)}) all-reduce(f32[2,4,128]{2,1,0:T(4,128)S(1)} %pad_maximum_fusion.10, f32[2,3,384]{2,1,0:T(4,128)S(1)} %pad_maximum_fusion.9), channel_id=1, replica_groups=mesh['seq'=8,'feat'=4] {'seq'}, use_global_device_ids=true, to_apply=%region_28.0 | all-reduce | flops 3328 | bytes 26624 | tf_op jit(solution)/shard_map/psum | solution.py:221
  1095.4 110.1 %all-reduce.330.cloned.1.call-done = (f32[2,128,768]{2,1,0:T(8,128)}, f32[2,1536,128]{2,1,0:T(8,128)}, f32[2,512,128]{2,1,0:T(8,128)}) async-done(((f32[2,128,768]{2,1,0:T(8,128)}, f32[2,1536,128]{2,1,0:T(8,128)}, f32[2,512,128]{2,1,0:T(8,128)}), (f32[2,128,768]{2,1,0:T(8,128)}, f32[2,1536,128]{2,1,0:T(8,128)}, f32[2,512,128]{2,1,0:T(8,128)})) %all-reduce.330.cloned.1.call-update) | async-done | bytes 2883600 | tf_op jit(solution)/shard_map/psum | solution.py:221
  1212.2 3.1 add_multiply_fusion
  (1597 shorter events, 422.5 us)
Async XLA Ops:
  7.2 25.5 %all-gather.7.cloned.1.call-start = ((), (), s32[]{:S(2)}) async-start(), calls=%async_computation.2 | async-start | bytes 1966080 | tf_op jit(solution)/shard_map/all_gather | solution.py:108
  9.0 86.5 %all-reduce.322.cloned.1.call-start = ((), (), s32[]{:S(2)}) async-start(), calls=%async_computation.3 | async-start | bytes 4718592 | tf_op jit(solution)/shard_map/psum | solution.py:125
  39.8 145.1 %all-gather.9.cloned.1.call-start = ((), (), s32[]{:S(2)}) async-start(), calls=%async_computation.4 | async-start | bytes 1966080 | tf_op jit(solution)/shard_map/all_gather | solution.py:108
  43.4 54.2 %copy-start.553 = (f32[384]{0:T(512)}, f32[384]{0:T(512)S(1)}, u32[]{:S(2)}) copy-start(f32[384]{0:T(512)S(1)} %get-tuple-element.706) | copy-start | bytes 4612
  43.4 54.2 %copy-start.555 = (f32[384]{0:T(512)}, f32[384]{0:T(512)S(1)}, u32[]{:S(2)}) copy-start(f32[384]{0:T(512)S(1)} %get-tuple-element.707) | copy-start | bytes 4612
  100.3 27.3 %copy-start.16 = (f32[768,384]{1,0:T(8,128)}, f32[768,384]{1,0:T(8,128)S(1)}, u32[]{:S(2)}) copy-start(f32[768,384]{1,0:T(8,128)S(1)} %get-tuple-element.600) | copy-start | bytes 3538948
  100.3 27.3 %copy-start.20 = (f32[768,384]{1,0:T(8,128)}, f32[768,384]{1,0:T(8,128)S(1)}, u32[]{:S(2)}) copy-start(f32[768,384]{1,0:T(8,128)S(1)} %get-tuple-element.599) | copy-start | bytes 3538948
  100.4 5.9 copy-start.122
  100.5 5.8 copy-start.124
  106.2 21.8 %copy-start = (f32[768,384]{1,0:T(8,128)}, f32[768,384]{1,0:T(8,128)S(1)}, u32[]{:S(2)}) copy-start(f32[768,384]{1,0:T(8,128)S(1)} %get-tuple-element.376) | copy-start | bytes 3538948
  106.2 21.8 %copy-start.2 = (f32[768,384]{1,0:T(8,128)}, f32[768,384]{1,0:T(8,128)S(1)}, u32[]{:S(2)}) copy-start(f32[768,384]{1,0:T(8,128)S(1)} %get-tuple-element.377) | copy-start | bytes 3538948
  106.2 22.6 %copy-start.24 = (f32[768,384]{1,0:T(8,128)}, f32[768,384]{1,0:T(8,128)S(1)}, u32[]{:S(2)}) copy-start(f32[768,384]{1,0:T(8,128)S(1)} %get-tuple-element.375) | copy-start | bytes 3538948
  125.3 19.5 %copy-start.148 = (f32[768,384]{1,0:T(8,128)}, f32[768,384]{1,0:T(8,128)S(1)}, u32[]{:S(2)}) copy-start(f32[768,384]{1,0:T(8,128)S(1)} %get-tuple-element.382) | copy-start | bytes 3538948
  125.4 19.5 %copy-start.150 = (f32[768,384]{1,0:T(8,128)}, f32[768,384]{1,0:T(8,128)S(1)}, u32[]{:S(2)}) copy-start(f32[768,384]{1,0:T(8,128)S(1)} %get-tuple-element.383) | copy-start | bytes 3538948
  143.9 5.4 copy-start.152
  143.9 5.4 copy-start.154
  143.9 5.3 copy-start.403
  153.9 10.5 copy-start.521
  154.0 10.5 copy-start.523
  164.4 83.3 %all-reduce.324.cloned.1.call-start = ((), (), s32[]{:S(2)}) async-start(), calls=%async_computation.5 | async-start | bytes 4718592 | tf_op jit(solution)/shard_map/psum | solution.py:125
  192.0 157.6 %reduce-scatter.3.cloned.1.call-start = ((), (), s32[]{:S(2)}) async-start(), calls=%async_computation.6 | async-start | bytes 1966080 | tf_op jit(solution)/shard_map/reduce_scatter | solution.py:199
  192.1 57.7 %copy-start.557 = (f32[384]{0:T(512)}, f32[384]{0:T(512)S(1)}, u32[]{:S(2)}) copy-start(f32[384]{0:T(512)S(1)} %get-tuple-element.700) | copy-start | bytes 4612
  192.1 57.7 %copy-start.559 = (f32[384]{0:T(512)}, f32[384]{0:T(512)S(1)}, u32[]{:S(2)}) copy-start(f32[384]{0:T(512)S(1)} %get-tuple-element.701) | copy-start | bytes 4612
  253.7 27.3 %copy-start.18 = (f32[768,384]{1,0:T(8,128)}, f32[768,384]{1,0:T(8,128)S(1)}, u32[]{:S(2)}) copy-start(f32[768,384]{1,0:T(8,128)S(1)} %get-tuple-element.602) | copy-start | bytes 3538948
  253.7 27.3 %copy-start.22 = (f32[768,384]{1,0:T(8,128)}, f32[768,384]{1,0:T(8,128)S(1)}, u32[]{:S(2)}) copy-start(f32[768,384]{1,0:T(8,128)S(1)} %get-tuple-element.601) | copy-start | bytes 3538948
  253.8 6.2 copy-start.126
  253.9 6.1 copy-start.128
  259.8 21.5 %copy-start.4 = (f32[768,384]{1,0:T(8,128)}, f32[768,384]{1,0:T(8,128)S(1)}, u32[]{:S(2)}) copy-start(f32[768,384]{1,0:T(8,128)S(1)} %get-tuple-element.320) | copy-start | bytes 3538948
  259.8 21.5 %copy-start.6 = (f32[768,384]{1,0:T(8,128)}, f32[768,384]{1,0:T(8,128)S(1)}, u32[]{:S(2)}) copy-start(f32[768,384]{1,0:T(8,128)S(1)} %get-tuple-element.321) | copy-start | bytes 3538948
  259.8 22.4 %copy-start.30 = (f32[768,384]{1,0:T(8,128)}, f32[768,384]{1,0:T(8,128)S(1)}, u32[]{:S(2)}) copy-start(f32[768,384]{1,0:T(8,128)S(1)} %get-tuple-element.319) | copy-start | bytes 3538948
  278.7 19.5 %copy-start.156 = (f32[768,384]{1,0:T(8,128)}, f32[768,384]{1,0:T(8,128)S(1)}, u32[]{:S(2)}) copy-start(f32[768,384]{1,0:T(8,128)S(1)} %get-tuple-element.326) | copy-start | bytes 3538948
  278.7 19.5 %copy-start.158 = (f32[768,384]{1,0:T(8,128)}, f32[768,384]{1,0:T(8,128)S(1)}, u32[]{:S(2)}) copy-start(f32[768,384]{1,0:T(8,128)S(1)} %get-tuple-element.327) | copy-start | bytes 3538948
  304.1 10.8 copy-start.529
  304.1 10.8 copy-start.589
  306.7 10.9 copy-start.549
  306.8 10.9 copy-start.550
  320.8 130.2 %all-reduce.326.cloned.1.call-start = ((), (), s32[]{:S(2)}) async-start(), calls=%async_computation.7 | async-start | bytes 9437184 | tf_op jit(solution)/shard_map/psum | solution.py:136
  356.8 322.2 %all-gather.13.cloned.1.call-start = ((), (), s32[]{:S(2)}) async-start(), calls=%async_computation.9 | async-start | bytes 1966080 | tf_op jit(solution)/shard_map/all_gather | solution.py:118
  451.0 9.3 copy-start.251
  467.7 5.1 copy-start.506
  471.3 18.4 %copy-start.349 = (f32[768,384]{1,0:T(8,128)}, f32[768,384]{1,0:T(8,128)S(1)}, u32[]{:S(2)}) copy-start(f32[768,384]{1,0:T(8,128)S(1)} %get-tuple-element.654) | copy-start | bytes 3538948
  658.9 42.2 %all-gather.11.cloned.1.call-start = ((), (), s32[]{:S(2)}) async-start(), calls=%async_computation.8 | async-start | bytes 1966080 | tf_op jit(solution)/shard_map/all_gather | solution.py:117
  659.6 76.4 %reduce-scatter.5.cloned.1.call-start = ((), (), s32[]{:S(2)}) async-start(), calls=%async_computation.10 | async-start | bytes 1966080 | tf_op jit(solution)/shard_map/reduce_scatter | solution.py:199
  679.0 23.7 %copy-start.530 = (bf16[768,128]{1,0:T(8,128)(2,1)S(1)}, bf16[768,128]{1,0:T(8,128)(2,1)}, u32[]{:S(2)}) copy-start(bf16[768,128]{1,0:T(8,128)(2,1)} %param.20) | copy-start | bytes 589828
  680.6 22.1 %copy-start.497 = (f32[768,128]{1,0:T(8,128)S(1)}, f32[768,128]{1,0:T(8,128)}, u32[]{:S(2)}) copy-start(f32[768,128]{1,0:T(8,128)} %get-tuple-element.682) | copy-start | bytes 1179652
  680.7 22.1 %copy-start.522 = (f32[768,128]{1,0:T(8,128)S(1)}, f32[768,128]{1,0:T(8,128)}, u32[]{:S(2)}) copy-start(f32[768,128]{1,0:T(8,128)} %copy-done.521) | copy-start | bytes 1179652
  680.7 22.1 %copy-start.524 = (f32[768,128]{1,0:T(8,128)S(1)}, f32[768,128]{1,0:T(8,128)}, u32[]{:S(2)}) copy-start(f32[768,128]{1,0:T(8,128)} %copy-done.523) | copy-start | bytes 1179652
  680.7 22.1 %copy-start.525 = (f32[768,128]{1,0:T(8,128)S(1)}, f32[768,128]{1,0:T(8,128)}, u32[]{:S(2)}) copy-start(f32[768,128]{1,0:T(8,128)} %get-tuple-element.727) | copy-start | bytes 1179652
  704.6 31.4 %copy-start.498 = (f32[768,128]{1,0:T(8,128)}, f32[768,128]{1,0:T(8,128)S(1)}, u32[]{:S(2)}) copy-start(f32[768,128]{1,0:T(8,128)S(1)} %get-tuple-element.286) | copy-start | bytes 1179652
  707.7 128.3 %all-reduce.328.cloned.1.call-start = ((), (), s32[]{:S(2)}) async-start(), calls=%async_computation.11 | async-start | bytes 9437184 | tf_op jit(solution)/shard_map/psum | solution.py:136
  741.8 94.2 %copy-start.450 = (f32[256,384]{1,0:T(8,128)S(1)}, f32[256,384]{1,0:T(8,128)}, u32[]{:S(2)}) copy-start(f32[256,384]{1,0:T(8,128)} %copy-done.449) | copy-start | bytes 1179652
  741.8 94.2 %copy-start.452 = (f32[256,384]{1,0:T(8,128)S(1)}, f32[256,384]{1,0:T(8,128)}, u32[]{:S(2)}) copy-start(f32[256,384]{1,0:T(8,128)} %copy-done.451) | copy-start | bytes 1179652
  741.8 348.1 %all-gather.17.cloned.1.call-start = ((), (), s32[]{:S(2)}) async-start(), calls=%async_computation.13 | async-start | bytes 1966080 | tf_op jit(solution)/shard_map/all_gather | solution.py:118
  836.0 8.8 copy-start.247
  1035.7 55.9 %all-gather.15.cloned.1.call-start = ((), (), s32[]{:S(2)}) async-start(), calls=%async_computation.12 | async-start | bytes 1966080 | tf_op jit(solution)/shard_map/all_gather | solution.py:117
  1036.3 169.1 %all-reduce.330.cloned.1.call-start = ((), (), s32[]{:S(2)}) async-start(), calls=%async_computation.14 | async-start | bytes 5767168 | tf_op jit(solution)/shard_map/psum | solution.py:221
  1048.5 38.4 %copy-start.563 = (f32[2,3,384]{2,0,1:T(2,128)S(1)}, f32[2,3,384]{2,0,1:T(2,128)}, u32[]{:S(2)}) copy-start(f32[2,3,384]{2,0,1:T(2,128)} %param.37) | copy-start | bytes 27652
  1048.5 38.4 %copy-start.564 = (f32[2,3,384]{2,0,1:T(2,128)S(1)}, f32[2,3,384]{2,0,1:T(2,128)}, u32[]{:S(2)}) copy-start(f32[2,3,384]{2,0,1:T(2,128)} %param.32) | copy-start | bytes 27652
  1048.5 40.8 %copy-start.562 = (f32[2,4,128]{2,1,0:T(4,128)S(1)}, f32[2,4,128]{2,1,0:T(4,128)}, u32[]{:S(2)}) copy-start(f32[2,4,128]{2,1,0:T(4,128)} %param.26) | copy-start | bytes 12292
  1048.5 40.8 %copy-start.577 = (f32[2,4,128]{2,1,0:T(4,128)S(1)}, f32[2,4,128]{2,1,0:T(4,128)}, u32[]{:S(2)}) copy-start(f32[2,4,128]{2,1,0:T(4,128)} %param.36) | copy-start | bytes 12292
  1048.5 40.8 %copy-start.578 = (f32[2,4,128]{2,1,0:T(4,128)S(1)}, f32[2,4,128]{2,1,0:T(4,128)}, u32[]{:S(2)}) copy-start(f32[2,4,128]{2,1,0:T(4,128)} %param.31) | copy-start | bytes 12292
  1091.6 113.9 %copy-start.515 = (f32[2,512,128]{2,1,0:T(8,128)S(1)}, f32[2,512,128]{2,1,0:T(8,128)}, u32[]{:S(2)}) copy-start(f32[2,512,128]{2,1,0:T(8,128)} %param.25) | copy-start | bytes 1572868
  1091.6 113.9 %copy-start.547 = (f32[2,512,128]{2,1,0:T(8,128)S(1)}, f32[2,512,128]{2,1,0:T(8,128)}, u32[]{:S(2)}) copy-start(f32[2,512,128]{2,1,0:T(8,128)} %param.35) | copy-start | bytes 1572868
  1091.6 113.9 %copy-start.548 = (f32[2,512,128]{2,1,0:T(8,128)S(1)}, f32[2,512,128]{2,1,0:T(8,128)}, u32[]{:S(2)}) copy-start(f32[2,512,128]{2,1,0:T(8,128)} %param.30) | copy-start | bytes 1572868
  (541 other events, 1082.5 us)
Sparse Core Ops, SparseCore 0:
  10.2 22.5 all-gather.6
  39.9 55.6 all-reduce.321
  164.6 20.2 all-gather.8
  192.1 55.6 all-reduce.323
  320.9 28.6 reduce-scatter.2
  356.9 94.0 all-reduce.325
  659.0 19.9 all-gather.12
  681.2 19.8 all-gather.10
  707.8 28.1 reduce-scatter.4
  742.0 94.0 all-reduce.327
  1035.9 19.9 all-gather.16
  1057.9 19.8 all-gather.14
  1082.3 123.1 all-reduce.329
where the time goes:
time: 1230 us; the launch traced here: 1220 us
  waiting for transfers between devices  546 us (44%)
  other arithmetic  391 us (32%)
  local copies, waits for them, and re-layouts  167 us (14%)
  blocking collectives  53.4 us (4%)
  matrix products  42.7 us (3%)
  between operations  20.4 us (2%)
    psum x2, waiting for transfers between devices, state_backward(): states_grad = lax.psum(partial_states, 'feat')  188 us
    unnamed x1188, local copies, waits for them, and re-layouts  153 us
    neg x32, other arithmetic, combine(): mult_real = later[0] * earlier[0] - later[1] * earlier[1]  115 us
    psum x1, waiting for transfers between devices, body(): lax.psum((stacked_in, stacked_out, stacked_gate, stacked_feature, stacked...  110 us
    psum x2, waiting for transfers between devices, state_forward(): drive = lax.psum(partial_drive, 'feat')  108 us
    add_any x40, other arithmetic, combine(): add_real = later[0] * earlier[2] - later[1] * earlier[3] + later[2]  59.8 us
    neg x36, other arithmetic, combine(): add_real = later[0] * earlier[2] - later[1] * earlier[3] + later[2]  58.3 us
    reduce_scatter x2, waiting for transfers between devices, body(): lax.psum_scatter(contract_cols(pre_grad, gate_low), 'feat', scatter_dimen...  57 us
  transfers between devices with their start and end apart: 13, of which 11 were waited for; matrix products, arithmetic and copies ran while one was open for 2% of the time, Pallas kernels for 0%

commit v1 on v0

--- a/solution.py
+++ b/solution.py
@@ -133,7 +133,7 @@
         return scan_states(drive_in, rows_in, masks[0], masks[1], masks[2])
 
     partial_states = contract_cols(mixed_low, out_low)
-    states_grad = lax.psum(partial_states, "feat")
+    states_grad = jnp.sum(lax.all_gather(partial_states, "feat"), axis=0)
     unused, pull = jax.vjp(scanned, drive, state_row)
     drive_grad, row_grad = pull(states_grad)
     return (drive_grad.astype(jnp.bfloat16), row_grad)

time: 1230 us -> 1310 us (1.065)
  waiting for transfers between devices: 546 us -> 598 us
  other arithmetic: 391 us -> 423 us
    all_gather x0 -> x2, waiting for transfers between devices: none -> 240 us  [state_backward(): states_grad = jnp.sum(lax.all_gather(partial_states, 'feat'), axis=0)]
    psum x2 -> x0, waiting for transfers between devices: 188 us -> none  [state_backward(): states_grad = lax.psum(partial_states, 'feat')]
    reduce_sum x0 -> x2, other arithmetic: none -> 22.5 us  [state_backward(): states_grad = jnp.sum(lax.all_gather(partial_states, 'feat'), axis=0)]
    unnamed x1188 -> x1168, local copies, waits for them, and re-layouts: 153 us -> 148 us
where the time goes in v1:
time: 1310 us; the launch traced here: 1300 us
  waiting for transfers between devices  598 us (46%)
  other arithmetic  423 us (32%)
  local copies, waits for them, and re-layouts  162 us (12%)
  blocking collectives  53.4 us (4%)
  matrix products  42.8 us (3%)
  between operations  20.2 us (2%)
    all_gather x2, waiting for transfers between devices, state_backward(): states_grad = jnp.sum(lax.all_gather(partial_states, 'feat'), axis=0)  240 us
    unnamed x1168, local copies, waits for them, and re-layouts  148 us
    neg x32, other arithmetic, combine(): mult_real = later[0] * earlier[0] - later[1] * earlier[1]  117 us
    psum x1, waiting for transfers between devices, body(): lax.psum((stacked_in, stacked_out, stacked_gate, stacked_feature, stacked...  110 us
    psum x2, waiting for transfers between devices, state_forward(): drive = lax.psum(partial_drive, 'feat')  108 us
    add_any x40, other arithmetic, combine(): add_real = later[0] * earlier[2] - later[1] * earlier[3] + later[2]  60.7 us
    neg x36, other arithmetic, combine(): add_real = later[0] * earlier[2] - later[1] * earlier[3] + later[2]  60.7 us
    reduce_scatter x2, waiting for transfers between devices, body(): lax.psum_scatter(contract_cols(pre_grad, gate_low), 'feat', scatter_dimen...  57 us
  transfers between devices with their start and end apart: 13, of which 11 were waited for; matrix products, arithmetic and copies ran while one was open for 2% of the time, Pallas kernels for 0%

profile of v1, /device:TPU:0, one launch (start us, length us, event | category | flops | bytes accessed | tf_op | source)
XLA Modules:
  0.0 1300.7 jit_solution(6664753887154520716)
XLA Ops:
  10.5 22.2 %all-gather.11.cloned.1.call-done = f32[768,512]{1,0:T(8,128)} async-done(((f32[768,128]{1,0:T(8,128)}), f32[768,512]{1,0:T(8,128)}) %all-gather.11.cloned.1.call-update) | async-done | bytes 1572880 | tf_op jit(solution)/shard_map/all_gather | solution.py:108
  36.7 3.1 fusion.344
  43.4 52.1 %all-reduce.320.cloned.1.call-done = f32[768,768]{1,0:T(8,128)} async-done(((f32[768,768]{1,0:T(8,128)}), f32[768,768]{1,0:T(8,128)}) %all-reduce.320.cloned.1.call-update) | async-done | bytes 2359312 | tf_op jit(solution)/shard_map/psum | solution.py:125
  103.3 2.9 subtract_add_fusion.23
  153.5 8.2 all_gather.37
  164.1 20.4 %all-gather.13.cloned.1.call-done = f32[768,512]{1,0:T(8,128)} async-done(((f32[768,128]{1,0:T(8,128)}), f32[768,512]{1,0:T(8,128)}) %all-gather.13.cloned.1.call-update) | async-done | bytes 1572880 | tf_op jit(solution)/shard_map/all_gather | solution.py:108
  188.4 3.1 fusion.345
  191.7 55.7 %all-reduce.322.cloned.1.call-done = f32[768,768]{1,0:T(8,128)} async-done(((f32[768,768]{1,0:T(8,128)}), f32[768,768]{1,0:T(8,128)}) %all-reduce.322.cloned.1.call-update) | async-done | bytes 2359312 | tf_op jit(solution)/shard_map/psum | solution.py:125
  256.2 3.1 subtract_add_fusion.11
  306.6 8.2 all_gather.39
  320.6 28.8 %reduce-scatter.3.cloned.1.call-done = f32[768,128]{1,0:T(8,128)} async-done(((f32[768,512]{1,0:T(8,128)}), f32[768,128]{1,0:T(8,128)}) %reduce-scatter.3.cloned.1.call-update) | async-done | bytes 393232 | tf_op jit(solution)/shard_map/reduce_scatter | solution.py:199
  352.7 3.9 fusion.341
  357.1 119.7 %all-gather.23.cloned.1.call-done = f32[3072,1536]{1,0:T(8,128)} async-done(((f32[768,1536]{1,0:T(8,128)}), f32[3072,1536]{1,0:T(8,128)}) %all-gather.23.cloned.1.call-update) | async-done | bytes 18874384 | tf_op jit(solution)/shard_map/all_gather | solution.py:136
  476.8 11.2 reduce_sum.303
  488.0 5.1 fusion.478
  493.2 2.9 fusion.328
  498.9 5.8 fusion.447
  504.7 3.6 fusion.502
  522.5 3.2 fusion.433
  534.5 3.6 fusion.445
  545.6 3.8 fusion.444
  557.9 3.8 fusion.432
  568.5 4.0 fusion.431
  579.0 3.3 fusion.443
  590.1 3.8 fusion.442
  602.2 4.0 fusion.430
  614.1 3.8 fusion.429
  625.8 4.0 fusion.441
  629.7 2.8 fusion.497
  638.9 4.0 fusion.440
  650.9 3.9 fusion.439
  661.4 4.2 multiply_reduce_fusion.3
  669.5 3.9 fusion.428
  678.8 2.9 fusion.427
  685.6 3.3 multiply_reduce_fusion.2
  695.6 3.0 multiply_reduce_fusion.19
  699.4 19.2 %all-gather.17.cloned.1.call-done = f32[768,512]{1,0:T(8,128)} async-done(((f32[768,128]{1,0:T(8,128)}), f32[768,512]{1,0:T(8,128)}) %all-gather.17.cloned.1.call-update) | async-done | bytes 1572880 | tf_op jit(solution)/shard_map/all_gather | solution.py:118
  720.3 20.4 %all-gather.15.cloned.1.call-done = f32[768,512]{1,0:T(8,128)} async-done(((f32[768,128]{1,0:T(8,128)}), f32[768,512]{1,0:T(8,128)}) %all-gather.15.cloned.1.call-update) | async-done | bytes 1572880 | tf_op jit(solution)/shard_map/all_gather | solution.py:117
  747.4 28.3 %reduce-scatter.5.cloned.1.call-done = f32[768,128]{1,0:T(8,128)} async-done(((f32[768,512]{1,0:T(8,128)}), f32[768,128]{1,0:T(8,128)}) %reduce-scatter.5.cloned.1.call-update) | async-done | bytes 393232 | tf_op jit(solution)/shard_map/reduce_scatter | solution.py:199
  777.6 3.9 fusion.340
  781.7 120.0 %all-gather.25.cloned.1.call-done = f32[3072,1536]{1,0:T(8,128)} async-done(((f32[768,1536]{1,0:T(8,128)}), f32[3072,1536]{1,0:T(8,128)}) %all-gather.25.cloned.1.call-update) | async-done | bytes 18874384 | tf_op jit(solution)/shard_map/all_gather | solution.py:136
  901.7 11.2 reduce_sum.309
  912.9 4.4 fusion.477
  917.3 2.9 fusion.324
  923.0 5.4 fusion.423
  928.4 3.6 fusion.486
  943.7 3.3 fusion.409
  963.2 3.9 fusion.420
  973.9 3.2 fusion.408
  984.6 4.0 fusion.407
  995.3 3.8 fusion.419
  1007.3 3.8 fusion.418
  1019.3 3.9 fusion.406
  1031.4 3.8 fusion.405
  1043.1 4.1 fusion.417
  1056.4 4.0 fusion.416
  1068.4 3.9 fusion.415
  1078.9 3.4 multiply_reduce_fusion.11
  1086.2 3.9 fusion.404
  1095.4 2.9 fusion.403
  1111.6 2.9 multiply_reduce_fusion.21
  1128.6 37.1 %all-reduce.314 = (f32[2,4,128]{2,1,0:T(4,128)S(1)}, f32[2,3,384]{2,1,0:T(4,128)S(1)}) all-reduce(f32[2,4,128]{2,1,0:T(4,128)S(1)} %pad_maximum_fusion.10, f32[2,3,384]{2,1,0:T(4,128)S(1)} %pad_maximum_fusion.9), channel_id=1, replica_groups=mesh['seq'=8,'feat'=4] {'seq'}, use_global_device_ids=true, to_apply=%region_28.0 | all-reduce | flops 3328 | bytes 26624 | tf_op jit(solution)/shard_map/psum | solution.py:221
  1174.1 110.0 %all-reduce.324.cloned.1.call-done = (f32[2,128,768]{2,1,0:T(8,128)}, f32[2,1536,128]{2,1,0:T(8,128)}, f32[2,512,128]{2,1,0:T(8,128)}) async-done(((f32[2,128,768]{2,1,0:T(8,128)}, f32[2,1536,128]{2,1,0:T(8,128)}, f32[2,512,128]{2,1,0:T(8,128)}), (f32[2,128,768]{2,1,0:T(8,128)}, f32[2,1536,128]{2,1,0:T(8,128)}, f32[2,512,128]{2,1,0:T(8,128)})) %all-reduce.324.cloned.1.call-update) | async-done | bytes 2883600 | tf_op jit(solution)/shard_map/psum | solution.py:221
  1290.9 3.1 add_multiply_fusion
  (1579 shorter events, 431.0 us)
Async XLA Ops:
  7.2 25.5 %all-gather.11.cloned.1.call-start = ((), (), s32[]{:S(2)}) async-start(), calls=%async_computation.2 | async-start | bytes 1966080 | tf_op jit(solution)/shard_map/all_gather | solution.py:108
  9.0 86.5 %all-reduce.320.cloned.1.call-start = ((), (), s32[]{:S(2)}) async-start(), calls=%async_computation.3 | async-start | bytes 4718592 | tf_op jit(solution)/shard_map/psum | solution.py:125
  39.8 144.7 %all-gather.13.cloned.1.call-start = ((), (), s32[]{:S(2)}) async-start(), calls=%async_computation.4 | async-start | bytes 1966080 | tf_op jit(solution)/shard_map/all_gather | solution.py:108
  43.4 54.2 %copy-start.543 = (f32[384]{0:T(512)}, f32[384]{0:T(512)S(1)}, u32[]{:S(2)}) copy-start(f32[384]{0:T(512)S(1)} %get-tuple-element.706) | copy-start | bytes 4612
  43.4 54.2 %copy-start.545 = (f32[384]{0:T(512)}, f32[384]{0:T(512)S(1)}, u32[]{:S(2)}) copy-start(f32[384]{0:T(512)S(1)} %get-tuple-element.707) | copy-start | bytes 4612
  100.3 27.3 %copy-start.18 = (f32[768,384]{1,0:T(8,128)}, f32[768,384]{1,0:T(8,128)S(1)}, u32[]{:S(2)}) copy-start(f32[768,384]{1,0:T(8,128)S(1)} %get-tuple-element.600) | copy-start | bytes 3538948
  100.3 27.3 %copy-start.22 = (f32[768,384]{1,0:T(8,128)}, f32[768,384]{1,0:T(8,128)S(1)}, u32[]{:S(2)}) copy-start(f32[768,384]{1,0:T(8,128)S(1)} %get-tuple-element.599) | copy-start | bytes 3538948
  100.4 5.9 copy-start.124
  100.5 5.8 copy-start.126
  106.2 21.8 %copy-start = (f32[768,384]{1,0:T(8,128)}, f32[768,384]{1,0:T(8,128)S(1)}, u32[]{:S(2)}) copy-start(f32[768,384]{1,0:T(8,128)S(1)} %get-tuple-element.376) | copy-start | bytes 3538948
  106.2 21.8 %copy-start.2 = (f32[768,384]{1,0:T(8,128)}, f32[768,384]{1,0:T(8,128)S(1)}, u32[]{:S(2)}) copy-start(f32[768,384]{1,0:T(8,128)S(1)} %get-tuple-element.377) | copy-start | bytes 3538948
  106.2 22.6 %copy-start.26 = (f32[768,384]{1,0:T(8,128)}, f32[768,384]{1,0:T(8,128)S(1)}, u32[]{:S(2)}) copy-start(f32[768,384]{1,0:T(8,128)S(1)} %get-tuple-element.375) | copy-start | bytes 3538948
  125.4 19.2 %copy-start.148 = (f32[768,384]{1,0:T(8,128)}, f32[768,384]{1,0:T(8,128)S(1)}, u32[]{:S(2)}) copy-start(f32[768,384]{1,0:T(8,128)S(1)} %get-tuple-element.382) | copy-start | bytes 3538948
  125.4 19.2 %copy-start.150 = (f32[768,384]{1,0:T(8,128)}, f32[768,384]{1,0:T(8,128)S(1)}, u32[]{:S(2)}) copy-start(f32[768,384]{1,0:T(8,128)S(1)} %get-tuple-element.383) | copy-start | bytes 3538948
  143.6 5.3 copy-start.152
  143.6 5.3 copy-start.154
  143.6 5.2 copy-start.389
  153.5 10.5 copy-start.511
  153.5 10.5 copy-start.513
  164.0 83.3 %all-reduce.322.cloned.1.call-start = ((), (), s32[]{:S(2)}) async-start(), calls=%async_computation.5 | async-start | bytes 4718592 | tf_op jit(solution)/shard_map/psum | solution.py:125
  191.5 157.8 %reduce-scatter.3.cloned.1.call-start = ((), (), s32[]{:S(2)}) async-start(), calls=%async_computation.6 | async-start | bytes 1966080 | tf_op jit(solution)/shard_map/reduce_scatter | solution.py:199
  191.6 57.7 %copy-start.547 = (f32[384]{0:T(512)}, f32[384]{0:T(512)S(1)}, u32[]{:S(2)}) copy-start(f32[384]{0:T(512)S(1)} %get-tuple-element.700) | copy-start | bytes 4612
  191.6 57.7 %copy-start.549 = (f32[384]{0:T(512)}, f32[384]{0:T(512)S(1)}, u32[]{:S(2)}) copy-start(f32[384]{0:T(512)S(1)} %get-tuple-element.701) | copy-start | bytes 4612
  253.2 27.4 %copy-start.20 = (f32[768,384]{1,0:T(8,128)}, f32[768,384]{1,0:T(8,128)S(1)}, u32[]{:S(2)}) copy-start(f32[768,384]{1,0:T(8,128)S(1)} %get-tuple-element.602) | copy-start | bytes 3538948
  253.2 27.4 %copy-start.24 = (f32[768,384]{1,0:T(8,128)}, f32[768,384]{1,0:T(8,128)S(1)}, u32[]{:S(2)}) copy-start(f32[768,384]{1,0:T(8,128)S(1)} %get-tuple-element.601) | copy-start | bytes 3538948
  253.3 6.1 copy-start.128
  253.4 6.1 copy-start.130
  259.3 21.7 %copy-start.4 = (f32[768,384]{1,0:T(8,128)}, f32[768,384]{1,0:T(8,128)S(1)}, u32[]{:S(2)}) copy-start(f32[768,384]{1,0:T(8,128)S(1)} %get-tuple-element.320) | copy-start | bytes 3538948
  259.3 21.7 %copy-start.6 = (f32[768,384]{1,0:T(8,128)}, f32[768,384]{1,0:T(8,128)S(1)}, u32[]{:S(2)}) copy-start(f32[768,384]{1,0:T(8,128)S(1)} %get-tuple-element.321) | copy-start | bytes 3538948
  259.3 22.5 %copy-start.32 = (f32[768,384]{1,0:T(8,128)}, f32[768,384]{1,0:T(8,128)S(1)}, u32[]{:S(2)}) copy-start(f32[768,384]{1,0:T(8,128)S(1)} %get-tuple-element.319) | copy-start | bytes 3538948
  278.3 19.6 %copy-start.156 = (f32[768,384]{1,0:T(8,128)}, f32[768,384]{1,0:T(8,128)S(1)}, u32[]{:S(2)}) copy-start(f32[768,384]{1,0:T(8,128)S(1)} %get-tuple-element.326) | copy-start | bytes 3538948
  278.3 19.6 %copy-start.158 = (f32[768,384]{1,0:T(8,128)}, f32[768,384]{1,0:T(8,128)S(1)}, u32[]{:S(2)}) copy-start(f32[768,384]{1,0:T(8,128)S(1)} %get-tuple-element.327) | copy-start | bytes 3538948
  303.9 10.9 copy-start.519
  303.9 10.9 copy-start.579
  306.5 10.9 copy-start.539
  306.5 10.9 copy-start.540
  320.5 156.2 %all-gather.23.cloned.1.call-start = ((), (), s32[]{:S(2)}) async-start(), calls=%async_computation.12 | async-start | bytes 23592960 | tf_op jit(solution)/shard_map/all_gather | solution.py:136
  356.6 362.0 %all-gather.17.cloned.1.call-start = ((), (), s32[]{:S(2)}) async-start(), calls=%async_computation.8 | async-start | bytes 1966080 | tf_op jit(solution)/shard_map/all_gather | solution.py:118
  488.0 9.3 copy-start.251
  504.7 5.2 copy-start.495
  661.4 5.3 copy-start.454
  698.6 42.1 %all-gather.15.cloned.1.call-start = ((), (), s32[]{:S(2)}) async-start(), calls=%async_computation.7 | async-start | bytes 1966080 | tf_op jit(solution)/shard_map/all_gather | solution.py:117
  699.4 76.2 %reduce-scatter.5.cloned.1.call-start = ((), (), s32[]{:S(2)}) async-start(), calls=%async_computation.9 | async-start | bytes 1966080 | tf_op jit(solution)/shard_map/reduce_scatter | solution.py:199
  718.6 23.7 %copy-start.520 = (bf16[768,128]{1,0:T(8,128)(2,1)S(1)}, bf16[768,128]{1,0:T(8,128)(2,1)}, u32[]{:S(2)}) copy-start(bf16[768,128]{1,0:T(8,128)(2,1)} %param.20) | copy-start | bytes 589828
  720.3 22.1 %copy-start.486 = (f32[768,128]{1,0:T(8,128)S(1)}, f32[768,128]{1,0:T(8,128)}, u32[]{:S(2)}) copy-start(f32[768,128]{1,0:T(8,128)} %get-tuple-element.682) | copy-start | bytes 1179652
  720.3 22.1 %copy-start.512 = (f32[768,128]{1,0:T(8,128)S(1)}, f32[768,128]{1,0:T(8,128)}, u32[]{:S(2)}) copy-start(f32[768,128]{1,0:T(8,128)} %copy-done.511) | copy-start | bytes 1179652
  720.3 22.1 %copy-start.514 = (f32[768,128]{1,0:T(8,128)S(1)}, f32[768,128]{1,0:T(8,128)}, u32[]{:S(2)}) copy-start(f32[768,128]{1,0:T(8,128)} %copy-done.513) | copy-start | bytes 1179652
  720.3 22.1 %copy-start.515 = (f32[768,128]{1,0:T(8,128)S(1)}, f32[768,128]{1,0:T(8,128)}, u32[]{:S(2)}) copy-start(f32[768,128]{1,0:T(8,128)} %get-tuple-element.727) | copy-start | bytes 1179652
  744.2 31.4 %copy-start.487 = (f32[768,128]{1,0:T(8,128)}, f32[768,128]{1,0:T(8,128)S(1)}, u32[]{:S(2)}) copy-start(f32[768,128]{1,0:T(8,128)S(1)} %get-tuple-element.286) | copy-start | bytes 1179652
  747.3 154.3 %all-gather.25.cloned.1.call-start = ((), (), s32[]{:S(2)}) async-start(), calls=%async_computation.13 | async-start | bytes 23592960 | tf_op jit(solution)/shard_map/all_gather | solution.py:136
  781.5 387.3 %all-gather.21.cloned.1.call-start = ((), (), s32[]{:S(2)}) async-start(), calls=%async_computation.11 | async-start | bytes 1966080 | tf_op jit(solution)/shard_map/all_gather | solution.py:118
  901.7 11.3 copy-start.438
  901.7 11.3 copy-start.440
  912.9 8.4 copy-start.247
  1114.6 55.8 %all-gather.19.cloned.1.call-start = ((), (), s32[]{:S(2)}) async-start(), calls=%async_computation.10 | async-start | bytes 1966080 | tf_op jit(solution)/shard_map/all_gather | solution.py:117
  1115.2 169.0 %all-reduce.324.cloned.1.call-start = ((), (), s32[]{:S(2)}) async-start(), calls=%async_computation.14 | async-start | bytes 5767168 | tf_op jit(solution)/shard_map/psum | solution.py:221
  1127.3 38.4 %copy-start.553 = (f32[2,3,384]{2,0,1:T(2,128)S(1)}, f32[2,3,384]{2,0,1:T(2,128)}, u32[]{:S(2)}) copy-start(f32[2,3,384]{2,0,1:T(2,128)} %param.37) | copy-start | bytes 27652
  1127.3 38.4 %copy-start.554 = (f32[2,3,384]{2,0,1:T(2,128)S(1)}, f32[2,3,384]{2,0,1:T(2,128)}, u32[]{:S(2)}) copy-start(f32[2,3,384]{2,0,1:T(2,128)} %param.32) | copy-start | bytes 27652
  1127.3 40.8 %copy-start.552 = (f32[2,4,128]{2,1,0:T(4,128)S(1)}, f32[2,4,128]{2,1,0:T(4,128)}, u32[]{:S(2)}) copy-start(f32[2,4,128]{2,1,0:T(4,128)} %param.26) | copy-start | bytes 12292
  1127.3 40.8 %copy-start.567 = (f32[2,4,128]{2,1,0:T(4,128)S(1)}, f32[2,4,128]{2,1,0:T(4,128)}, u32[]{:S(2)}) copy-start(f32[2,4,128]{2,1,0:T(4,128)} %param.36) | copy-start | bytes 12292
  1127.3 40.8 %copy-start.568 = (f32[2,4,128]{2,1,0:T(4,128)S(1)}, f32[2,4,128]{2,1,0:T(4,128)}, u32[]{:S(2)}) copy-start(f32[2,4,128]{2,1,0:T(4,128)} %param.31) | copy-start | bytes 12292
  1170.4 113.8 %copy-start.505 = (f32[2,512,128]{2,1,0:T(8,128)S(1)}, f32[2,512,128]{2,1,0:T(8,128)}, u32[]{:S(2)}) copy-start(f32[2,512,128]{2,1,0:T(8,128)} %param.25) | copy-start | bytes 1572868
  1170.4 113.8 %copy-start.537 = (f32[2,512,128]{2,1,0:T(8,128)S(1)}, f32[2,512,128]{2,1,0:T(8,128)}, u32[]{:S(2)}) copy-start(f32[2,512,128]{2,1,0:T(8,128)} %param.35) | copy-start | bytes 1572868
  1170.4 113.8 %copy-start.538 = (f32[2,512,128]{2,1,0:T(8,128)S(1)}, f32[2,512,128]{2,1,0:T(8,128)}, u32[]{:S(2)}) copy-start(f32[2,512,128]{2,1,0:T(8,128)} %param.30) | copy-start | bytes 1572868
  (531 other events, 1060.9 us)
Sparse Core Ops, SparseCore 0:
  10.2 22.5 all-gather.10
  39.9 55.6 all-reduce.319
  164.2 20.2 all-gather.12
  191.7 55.6 all-reduce.321
  320.7 28.6 reduce-scatter.2
  356.7 120.0 all-gather.22
  698.8 19.8 all-gather.16
  720.8 19.8 all-gather.14
  747.4 28.1 reduce-scatter.4
  781.6 120.0 all-gather.24
  1114.7 19.8 all-gather.20
  1136.6 19.8 all-gather.18
  1161.0 123.1 all-reduce.323
